TPU v7x, 256 devices: a whole 4x4x8 slice. The times are simulated.
256 devices in a mesh: ia: 8 (over y, core), ja: 8 (over z), ka: 4 (over x).
Axes of the slice: x: 4, y: 4, z: 8, core: 2. Of those that a mesh axis runs over, the one named last changes fastest.
Arguments:
- blocks: bfloat16 [256, 64, 64, 128], P(('ia', 'ja', 'ka')), may hold values from -6 to 6
- coords: int32 [3, 256], P(None, ('ia', 'ja', 'ka')), may hold values from 0 to 31, as said below
- live: int32 [256], P(('ia', 'ja', 'ka')), may hold values from 1 to 1, as said below
- factor_b: float32 [2048, 128], P('ja'), may hold values from -0.9 to 12
- factor_c: float32 [2048, 128], P('ka'), may hold values from -0.9 to 12
Outputs:
- loading_a: float32 [2048, 128], P('ia')
- loading_b: float32 [2048, 128], P('ja')
- loading_c: float32 [2048, 128], P('ka')
Inputs may be any that keep to these rules, and one draw needn't show every extreme that they name: `live`: slot d holds the block of device d (devices counted along ia, ja, ka, ia slowest). The slots of device (p, q, s) name blocks with coords[0] from p * 4 to p * 4 + 3, coords[1] from q * 4 to q * 4 + 3, coords[2] from s * 4 to s * 4 + 3; each device's slot names one block of its own 4 x 4 x 4 block region.
All inputs are finite; a program needn't handle non-finite values.
Results may differ from a plain program's by a relative error of at most 0.0057.
Values sent between devices are 32-bit elements; how exact they have to be, the bound alone decides.
No kernel may reach another device: no remote copies, remote signals or barrier semaphores. Data moves between devices by JAX's collectives and lax.ppermute only.
A program may use at most 64 MiB of HBM per device.

v0:
```python
import jax
import jax.numpy as jnp
from jax import lax
from jax.sharding import PartitionSpec as P

RANK = 128
BI = 64
BJ = 64
BK = 128
GI_DEV = 4
GJ_DEV = 4
GK_DEV = 4
RIDGE_SHARE = 0.3
EPSILON = 1e-06
HIGHEST = lax.Precision.HIGHEST
sweep_order = (0, 1, 2)


def factorize(gram_one, gram_two):
    merged = gram_one * gram_two
    order_rank = merged.shape[0]
    shift_value = RIDGE_SHARE * jnp.trace(merged) / order_rank
    lower_factor = jnp.linalg.cholesky(
        merged + shift_value * jnp.eye(order_rank, dtype=jnp.float32)
    )
    return lax.linalg.triangular_solve(
        lower_factor, jnp.eye(order_rank, dtype=jnp.float32), left_side=True, lower=True
    )


def apply_inverse(inverse_lower, values):
    middle = jnp.dot(values, inverse_lower.T, precision=HIGHEST, preferred_element_type=jnp.float32)
    return jnp.dot(middle, inverse_lower, precision=HIGHEST, preferred_element_type=jnp.float32)


def square_product(values):
    return jnp.dot(values.T, values, precision=HIGHEST, preferred_element_type=jnp.float32)


def grand_sum(values):
    return lax.psum(values, ("ia", "ja", "ka"))


def move_rows(mode_now, action, values):
    if mode_now == 0:
        if action == "reduce":
            return lax.psum_scatter(values, ("ja", "ka"), scatter_dimension=0, tiled=True)
        return lax.all_gather(values, ("ja", "ka"), axis=0, tiled=True)
    if mode_now == 1:
        if action == "reduce":
            return lax.psum_scatter(values, ("ia", "ka"), scatter_dimension=0, tiled=True)
        return lax.all_gather(values, ("ia", "ka"), axis=0, tiled=True)
    if action == "reduce":
        return lax.psum_scatter(values, ("ia", "ja"), scatter_dimension=0, tiled=True)
    return lax.all_gather(values, ("ia", "ja"), axis=0, tiled=True)


def group_place(mode_now):
    if mode_now == 0:
        return (lax.axis_index(("ja", "ka")), lax.axis_size(("ja", "ka")), lax.axis_size("ia"))
    if mode_now == 1:
        return (lax.axis_index(("ia", "ka")), lax.axis_size(("ia", "ka")), lax.axis_size("ja"))
    return (lax.axis_index(("ia", "ja")), lax.axis_size(("ia", "ja")), lax.axis_size("ka"))


def share_rows(values, group_index, group_size):
    share_width = values.shape[0] // group_size
    return lax.dynamic_slice_in_dim(values, group_index * share_width, share_width, 0)


def starting_gram(values, mode_now):
    group_index, group_size, mode_size = group_place(mode_now)
    share = share_rows(values, group_index, group_size)
    return grand_sum(square_product(share)) / (values.shape[0] * mode_size)


def normalize(stat_rows, count_rows, need_gram):
    squares = lax.psum(jnp.sum(stat_rows * stat_rows, axis=0), ("ia", "ja", "ka")) / count_rows
    scale = lax.rsqrt(squares + EPSILON)
    if not need_gram:
        return (scale, None)
    scaled = stat_rows * scale
    return (scale, grand_sum(square_product(scaled)) / count_rows)


def settle(mode_now, summed, inverse_lower, need_gram):
    group_index, group_size, mode_size = group_place(mode_now)
    count_rows = summed.shape[0] * mode_size
    solved = apply_inverse(inverse_lower, move_rows(mode_now, "reduce", summed))
    scale, gram_new = normalize(solved, count_rows, need_gram)
    return (move_rows(mode_now, "spread", solved * scale), gram_new)


def block_product(mode_now, tensor_block, rows_one, rows_two):
    khatri = (rows_one[:, None, :] * rows_two[None, :, :]).astype(jnp.bfloat16)
    kept_dims = tuple((axis_id for axis_id in range(3) if axis_id != mode_now))
    return lax.dot_general(
        tensor_block, khatri, ((kept_dims, (0, 1)), ((), ())), preferred_element_type=jnp.float32
    )


def local_mttkrp(mode_now, blocks, coords, live_count, factors, bases):
    extents = (BI, BJ, BK)
    spans = (BI * GI_DEV, BJ * GJ_DEV, BK * GK_DEV)
    others = tuple((axis_id for axis_id in range(3) if axis_id != mode_now))

    def visit(slot_index, summed):
        tensor_block = lax.dynamic_index_in_dim(blocks, slot_index, 0, keepdims=False)
        start_one = (coords[others[0], slot_index] - bases[others[0]]) * extents[others[0]]
        start_two = (coords[others[1], slot_index] - bases[others[1]]) * extents[others[1]]
        rows_one = lax.dynamic_slice_in_dim(factors[others[0]], start_one, extents[others[0]], 0)
        rows_two = lax.dynamic_slice_in_dim(factors[others[1]], start_two, extents[others[1]], 0)
        product_rows = block_product(mode_now, tensor_block, rows_one, rows_two)
        offset = (coords[mode_now, slot_index] - bases[mode_now]) * extents[mode_now]
        current = lax.dynamic_slice_in_dim(summed, offset, extents[mode_now], 0)
        return lax.dynamic_update_slice_in_dim(summed, current + product_rows, offset, 0)

    start_rows = jnp.zeros((spans[mode_now], RANK), jnp.float32)
    return lax.fori_loop(0, live_count, visit, start_rows)


def on_device(blocks, coords, live, factor_b, factor_c):
    bases = (
        lax.axis_index("ia") * GI_DEV,
        lax.axis_index("ja") * GJ_DEV,
        lax.axis_index("ka") * GK_DEV,
    )
    factors = [None, factor_b, factor_c]
    gram_list = [None, starting_gram(factor_b, 1), starting_gram(factor_c, 2)]
    for position, mode_now in enumerate(sweep_order):
        others = tuple((axis_id for axis_id in range(3) if axis_id != mode_now))
        summed = local_mttkrp(mode_now, blocks, coords, live[0], factors, bases)
        inverse_lower = factorize(gram_list[others[0]], gram_list[others[1]])
        factors[mode_now], gram_list[mode_now] = settle(
            mode_now, summed, inverse_lower, position < 2
        )
    return (factors[0], factors[1], factors[2])


def solution(mesh):
    placed = (
        P(("ia", "ja", "ka"), None, None, None),
        P(None, ("ia", "ja", "ka")),
        P(("ia", "ja", "ka")),
        P("ja", None),
        P("ka", None),
    )
    return jax.shard_map(
        on_device,
        mesh=mesh,
        in_specs=placed,
        out_specs=(P("ia", None), P("ja", None), P("ka", None)),
        check_vma=False,
    )
```

profile of v0, /device:TPU:2, one launch (start us, length us, event | category | flops | bytes accessed | tf_op | source)
XLA Modules:
  0.0 1532.1 jit_solution(2056919965706999280)
XLA Ops:
  7.2 1.7 fusion.37
  8.9 0.9 fusion.35
  9.9 1.4 fusion.46
  13.3 0.8 constant_dynamic-slice_fusion.3
  14.1 2.0 fusion.10
  16.1 1.4 while.42
  17.5 0.6 copy-done.2
  18.3 0.6 dynamic-slice.4
  18.9 0.6 dynamic-slice.2
  20.8 0.6 dynamic-slice
  22.0 241.3 %all-reduce.21.cloned.1.call-done = (f32[128,128]{0,1:T(8,128)}, f32[128,128]{0,1:T(8,128)}) async-done(((f32[128,128]{0,1:T(8,128)}, f32[128,128]{0,1:T(8,128)}), (f32[128,128]{0,1:T(8,128)}, f32[128,128]{0,1:T(8,128)})) %all-reduce.21.cloned.1.call-update) | async-done | bytes 131088 | tf_op jit(solution)/shard_map/psum | solution.py:41
  263.3 1.5 select_reduce_fusion.5
  265.4 0.9 select_add_fusion.2
  266.3 0.1 copy.17
  266.4 11.7 cholesky.59
  278.2 0.6 compare_reduce_fusion.2
  278.8 0.7 fusion.20
  279.5 9.8 custom-call.7
  289.3 0.3 fusion.18
  289.6 117.0 %all-reduce.15.cloned.1.call-done = f32[256,128]{1,0:T(8,128)} async-done(((f32[256,128]{1,0:T(8,128)}), f32[256,128]{1,0:T(8,128)}) %all-reduce.15.cloned.1.call-update) | async-done | bytes 131088
  406.6 0.8 fusion.33
  407.4 0.2 multiply_reduce_fusion.2
  407.6 73.5 %psum.51 = f32[128]{0:T(128)S(1)} all-reduce(f32[128]{0:T(128)S(1)} %get-tuple-element.553), channel_id=1, replica_groups=mesh['ia'=8,'ja'=8,'ka'=4] {'ia','ja','ka'}, use_global_device_ids=true, to_apply=%region_9.12 | all-reduce | flops 128 | bytes 1024 | tf_op jit(solution)/shard_map/psum | solution.py:78
  481.2 0.9 fusion.47
  482.1 41.7 %all_gather.9 = f32[256,128]{1,0:T(8,128)S(1)} all-gather(f32[8,128]{1,0:T(8,128)S(1)} %broadcast_multiply_fusion.2), channel_id=1, replica_groups=mesh['ia'=8,'ja'=8,'ka'=4] {'ja','ka'}, dimensions={0}, use_global_device_ids=true | all-gather | bytes 135168 | tf_op jit(solution)/shard_map/all_gather | solution.py:48
  523.9 0.5 fusion.9
  524.4 1.3 while.43
  525.7 0.6 copy-done.3
  526.4 0.2 all-reduce.13.cloned.1.call-start
  526.6 235.3 %all-reduce.11.cloned.1.call-done = f32[128,128]{0,1:T(8,128)} async-done(((f32[128,128]{0,1:T(8,128)}), f32[128,128]{0,1:T(8,128)}) %all-reduce.11.cloned.1.call-update) | async-done | bytes 65552 | tf_op jit(solution)/shard_map/psum | solution.py:41
  761.9 1.5 select_reduce_fusion.4
  764.0 0.9 select_add_fusion.1
  764.9 0.1 copy.19
  765.0 11.7 cholesky.70
  776.7 0.6 compare_reduce_fusion.1
  777.4 0.7 fusion.21
  778.0 9.8 custom-call.8
  787.9 0.3 fusion.16
  788.1 85.7 %all-reduce.17.cloned.1.call-done = f32[256,128]{1,0:T(8,128)} async-done(((f32[256,128]{1,0:T(8,128)}), f32[256,128]{1,0:T(8,128)}) %all-reduce.17.cloned.1.call-update) | async-done | bytes 131088
  873.9 0.8 fusion.31
  874.7 0.2 multiply_reduce_fusion.1
  875.0 75.7 %psum.53 = f32[128]{0:T(128)S(1)} all-reduce(f32[128]{0:T(128)S(1)} %get-tuple-element.555), channel_id=1, replica_groups=mesh['ia'=8,'ja'=8,'ka'=4] {'ia','ja','ka'}, use_global_device_ids=true, to_apply=%region_16.19 | all-reduce | flops 128 | bytes 1024 | tf_op jit(solution)/shard_map/psum | solution.py:78
  950.7 0.9 fusion.48
  951.6 33.7 %all_gather.10 = f32[256,128]{1,0:T(8,128)S(1)} all-gather(f32[8,128]{1,0:T(8,128)S(1)} %broadcast_multiply_fusion.1), channel_id=1, replica_groups=mesh['ia'=8,'ja'=8,'ka'=4] {'ia','ka'}, dimensions={0}, use_global_device_ids=true | all-gather | bytes 135168 | tf_op jit(solution)/shard_map/all_gather | solution.py:52
  985.4 0.5 convolution_bitcast_fusion
  986.0 1.6 while.44
  987.6 0.7 copy-done.1
  988.3 236.1 %all-reduce.13.cloned.1.call-done = f32[128,128]{0,1:T(8,128)} async-done(((f32[128,128]{0,1:T(8,128)}), f32[128,128]{0,1:T(8,128)}) %all-reduce.13.cloned.1.call-update) | async-done | bytes 65552 | tf_op jit(solution)/shard_map/psum | solution.py:41
  1224.4 1.5 select_reduce_fusion.3
  1226.5 0.9 select_add_fusion
  1227.4 0.1 copy.21
  1227.5 11.7 cholesky.81
  1239.2 0.6 compare_reduce_fusion
  1239.9 0.7 fusion.22
  1240.5 9.8 custom-call.9
  1250.3 0.3 fusion.14
  1250.6 151.3 %all-reduce.19.cloned.1.call-done = f32[512,128]{1,0:T(8,128)} async-done(((f32[512,128]{1,0:T(8,128)}), f32[512,128]{1,0:T(8,128)}) %all-reduce.19.cloned.1.call-update) | async-done | bytes 262160
  1401.9 0.9 fusion.29
  1402.7 0.2 multiply_reduce_fusion
  1403.0 75.0 %psum.55 = f32[128]{0:T(128)S(1)} all-reduce(f32[128]{0:T(128)S(1)} %get-tuple-element.557), channel_id=1, replica_groups=mesh['ia'=8,'ja'=8,'ka'=4] {'ia','ja','ka'}, use_global_device_ids=true, to_apply=%region_23.26 | all-reduce | flops 128 | bytes 1024 | tf_op jit(solution)/shard_map/psum | solution.py:78
  1477.9 45.3 %all_gather.11 = f32[512,128]{1,0:T(8,128)S(1)} all-gather(f32[8,128]{1,0:T(8,128)S(1)} %broadcast_multiply_fusion), channel_id=1, replica_groups=mesh['ia'=8,'ja'=8,'ka'=4] {'ia','ja'}, dimensions={0}, use_global_device_ids=true | all-gather | bytes 266240 | tf_op jit(solution)/shard_map/all_gather | solution.py:55
  1523.3 0.7 copy.62
  1523.9 0.7 copy.63
  1524.6 0.7 copy.64
  (49 shorter events, 0.7 us)
Async XLA Ops:
  7.2 1.8 copy-start
  7.2 256.1 %all-reduce.21.cloned.1.call-start = ((), (), s32[]{:S(2)}) async-start(), calls=%async_computation.5 | async-start | bytes 262144 | tf_op jit(solution)/shard_map/psum | solution.py:41
  9.9 396.7 %all-reduce.15.cloned.1.call-start = ((), (), s32[]{:S(2)}) async-start(), calls=%async_computation.2 | async-start | bytes 262144
  14.0 4.2 copy-start.9
  14.0 4.9 copy-start.8
  14.1 6.7 copy-start.7
  16.1 507.8 %copy-start.6 = (bf16[1,64,64,128]{3,2,1,0:T(8,128)(2,1)S(1)}, bf16[1,64,64,128]{3,2,1,0:T(8,128)(2,1)}, u32[]{:S(2)}) copy-start(bf16[1,64,64,128]{3,2,1,0:T(8,128)(2,1)} %param.14) | copy-start | bytes 3145732
  17.5 0.7 copy-start.2
  18.2 743.7 %all-reduce.11.cloned.1.call-start = ((), (), s32[]{:S(2)}) async-start(), calls=%async_computation | async-start | bytes 131072 | tf_op jit(solution)/shard_map/psum | solution.py:41
  523.8 350.1 %all-reduce.17.cloned.1.call-start = ((), (), s32[]{:S(2)}) async-start(), calls=%async_computation.3 | async-start | bytes 262144
  523.9 238.0 %copy-start.4 = (f32[128,128]{0,1:T(8,128)S(1)}, f32[128,128]{0,1:T(8,128)}, u32[]{:S(2)}) copy-start(f32[128,128]{0,1:T(8,128)} %get-tuple-element.548) | copy-start | bytes 196612
  525.7 0.7 copy-start.3
  526.4 698.0 %all-reduce.13.cloned.1.call-start = ((), (), s32[]{:S(2)}) async-start(), calls=%async_computation.1 | async-start | bytes 131072 | tf_op jit(solution)/shard_map/psum | solution.py:41
  985.4 416.5 %all-reduce.19.cloned.1.call-start = ((), (), s32[]{:S(2)}) async-start(), calls=%async_computation.4 | async-start | bytes 524288
  986.0 238.4 %copy-start.5 = (f32[128,128]{0,1:T(8,128)S(1)}, f32[128,128]{0,1:T(8,128)}, u32[]{:S(2)}) copy-start(f32[128,128]{0,1:T(8,128)} %all-reduce.11.cloned.1.call-done) | copy-start | bytes 196612
  987.6 0.7 copy-start.1
Sparse Core Ops, SparseCore 0:
  14.2 249.0 all-reduce.20
  267.3 139.2 all-reduce.14
  523.9 237.9 all-reduce.10
  765.5 108.3 all-reduce.16
  985.5 238.8 all-reduce.12
  1228.3 173.5 all-reduce.18
where the time goes:
time: 1530 us
  waiting for transfers between devices  1070 us (70%)
  blocking collectives  345 us (23%)
  other arithmetic  75.7 us (5%)
  between operations  20.2 us (1%)
    psum x3, waiting for transfers between devices, grand_sum(): return lax.psum(values, ('ia', 'ja', 'ka'))  713 us
    unnamed x9, waiting for transfers between devices  354 us
    psum x3, blocking collectives, normalize(): lax.psum(jnp.sum(stat_rows * stat_rows, axis=0), ('ia', 'ja', 'ka'))  224 us
    all_gather x1, blocking collectives, move_rows(): return lax.all_gather(values, ('ia', 'ja'), axis=0, tiled=True)  45.3 us
    all_gather x1, blocking collectives, move_rows(): return lax.all_gather(values, ('ja', 'ka'), axis=0, tiled=True)  41.7 us
    another operation x9, other arithmetic, factorize(): jnp.linalg.cholesky(merged + shift_value * jnp.eye(order_rank, dtype=jnp....  37.2 us
    all_gather x1, blocking collectives, move_rows(): return lax.all_gather(values, ('ia', 'ka'), axis=0, tiled=True)  33.7 us
    another operation x6, other arithmetic, factorize(): lax.linalg.triangular_solve(lower_factor, jnp.eye(order_rank, dtype=jnp.f...  31.4 us
  transfers between devices with their start and end apart: 6, of which 6 were waited for; matrix products, arithmetic and copies ran while one was open for 5% of the time, Pallas kernels for 0%

commit v1 on v0

--- a/solution.py
+++ b/solution.py
@@ -38,7 +38,7 @@
 
 
 def grand_sum(values):
-    return lax.psum(values, ("ia", "ja", "ka"))
+    return jnp.sum(lax.all_gather(values, ("ia", "ja", "ka")), axis=0)
 
 
 def move_rows(mode_now, action, values):

time: 1530 us -> 972 us (0.64)
  waiting for transfers between devices: 1070 us -> 480 us
  other arithmetic: 75.7 us -> 97.1 us
    psum x3 -> x0, waiting for transfers between devices: 713 us -> none  [grand_sum(): return lax.psum(values, ('ia', 'ja', 'ka'))]
    all_gather x0 -> x4, waiting for transfers between devices: none -> 401 us  [grand_sum(): return jnp.sum(lax.all_gather(values, ('ia', 'ja', 'ka')), axis=0)]
    unnamed x9 -> x10, waiting for transfers between devices: 354 us -> 79 us
    reduce_sum x0 -> x4, other arithmetic: none -> 26.5 us  [grand_sum(): return jnp.sum(lax.all_gather(values, ('ia', 'ja', 'ka')), axis=0)]
  transfers between devices with their start and end apart: 6 -> 7, of which waited for: 6 -> 6; matrix products, arithmetic and copies ran while one was open for 5% -> 11% of each run, Pallas kernels for 0% -> 0%
where the time goes in v1:
time: 972 us; the launch traced here: 971 us
  waiting for transfers between devices  480 us (49%)
  blocking collectives  347 us (36%)
  other arithmetic  97.1 us (10%)
  between operations  21.7 us (2%)
  matrix products  11.5 us (1%)
    all_gather x4, waiting for transfers between devices, grand_sum(): return jnp.sum(lax.all_gather(values, ('ia', 'ja', 'ka')), axis=0)  401 us
    psum x3, blocking collectives, normalize(): lax.psum(jnp.sum(stat_rows * stat_rows, axis=0), ('ia', 'ja', 'ka'))  225 us
    unnamed x10, waiting for transfers between devices  79 us
    all_gather x1, blocking collectives, move_rows(): return lax.all_gather(values, ('ia', 'ja'), axis=0, tiled=True)  45.3 us
    all_gather x1, blocking collectives, move_rows(): return lax.all_gather(values, ('ja', 'ka'), axis=0, tiled=True)  41.7 us
    another operation x9, other arithmetic, factorize(): jnp.linalg.cholesky(merged + shift_value * jnp.eye(order_rank, dtype=jnp....  37.2 us
    all_gather x1, blocking collectives, move_rows(): return lax.all_gather(values, ('ia', 'ka'), axis=0, tiled=True)  34.9 us
    another operation x6, other arithmetic, factorize(): lax.linalg.triangular_solve(lower_factor, jnp.eye(order_rank, dtype=jnp.f...  31.4 us
  transfers between devices with their start and end apart: 7, of which 6 were waited for; matrix products, arithmetic and copies ran while one was open for 11% of the time, Pallas kernels for 0%

profile of v1, /device:TPU:2, one launch (start us, length us, event | category | flops | bytes accessed | tf_op | source)
XLA Modules:
  0.0 971.1 jit_solution(4985701226535816155)
XLA Ops:
  8.1 1.7 fusion.37
  9.9 0.9 fusion.35
  10.9 1.4 fusion.46
  14.3 0.8 constant_dynamic-slice_fusion.3
  15.1 2.0 fusion.10
  17.1 1.3 while.42
  18.4 0.6 copy-done.3
  19.2 0.6 dynamic-slice
  20.3 121.4 %all-gather.9.cloned.1.call-done = f32[32768,128]{1,0:T(8,128)} async-done(((f32[128,128]{1,0:T(8,128)}), f32[32768,128]{1,0:T(8,128)}) %all-gather.9.cloned.1.call-update) | async-done | bytes 16777232 | tf_op jit(solution)/shard_map/all_gather | solution.py:41
  141.8 6.6 reduce_sum.85
  148.4 119.9 %all-gather.11.cloned.1.call-done = f32[32768,128]{1,0:T(8,128)} async-done(((f32[128,128]{1,0:T(8,128)}), f32[32768,128]{1,0:T(8,128)}) %all-gather.11.cloned.1.call-update) | async-done | bytes 16777232 | tf_op jit(solution)/shard_map/all_gather | solution.py:41
  268.3 6.7 reduce_sum.86
  275.1 0.6 select_reduce_fusion.5
  276.4 0.1 copy.13
  276.5 11.7 %cholesky.59 = f32[128,128]{1,0:T(8,128)S(1)} custom-call(f32[128,128]{1,0:T(8,128)S(1)} %fusion.28), custom_call_target="Cholesky" | custom-call | tf_op jit(solution)/shard_map/jit(cholesky)/cholesky | solution.py:23
  288.3 0.6 compare_reduce_fusion.2
  288.9 0.7 fusion.20
  289.6 9.8 %custom-call.7 = f32[1,128,128]{1,2,0:T(8,128)S(1)} custom-call(f32[1,128,128]{2,1,0:T(8,128)S(1)} %fusion.20), custom_call_target="InvertDiagBlocksLowerTriangular" | custom-call | tf_op jit(solution)/shard_map/triangular_solve/custom-call.0 | solution.py:26
  299.4 0.3 fusion.18
  299.7 0.8 fusion.33
  300.6 0.2 multiply_reduce_fusion.2
  300.8 74.4 %psum.21 = f32[128]{0:T(128)S(1)} all-reduce(f32[128]{0:T(128)S(1)} %get-tuple-element.551), channel_id=1, replica_groups=mesh['ia'=8,'ja'=8,'ka'=4] {'ia','ja','ka'}, use_global_device_ids=true, to_apply=%region_9.12 | all-reduce | flops 128 | bytes 1024 | tf_op jit(solution)/shard_map/psum | solution.py:78
  375.2 0.9 fusion.47
  376.2 0.6 dynamic-slice.2
  377.4 41.7 %all_gather.37 = f32[256,128]{1,0:T(8,128)S(1)} all-gather(f32[8,128]{1,0:T(8,128)S(1)} %broadcast_multiply_fusion.2), channel_id=1, replica_groups=mesh['ia'=8,'ja'=8,'ka'=4] {'ja','ka'}, dimensions={0}, use_global_device_ids=true | all-gather | bytes 135168 | tf_op jit(solution)/shard_map/all_gather | solution.py:48
  419.2 0.5 fusion.9
  419.7 1.3 while.43
  421.0 0.6 copy-done.4
  421.8 76.4 %all-gather.13.cloned.1.call-done = f32[32768,128]{1,0:T(8,128)} async-done(((f32[128,128]{1,0:T(8,128)}), f32[32768,128]{1,0:T(8,128)}) %all-gather.13.cloned.1.call-update) | async-done | bytes 16777232 | tf_op jit(solution)/shard_map/all_gather | solution.py:41
  498.2 6.6 reduce_sum.89
  504.8 0.1 copy.14
  504.9 0.6 select_reduce_fusion.4
  506.3 11.7 %cholesky.70 = f32[128,128]{1,0:T(8,128)S(1)} custom-call(f32[128,128]{1,0:T(8,128)S(1)} %fusion.26), custom_call_target="Cholesky" | custom-call | tf_op jit(solution)/shard_map/jit(cholesky)/cholesky | solution.py:23
  518.1 0.6 compare_reduce_fusion.1
  518.7 0.7 fusion.21
  519.4 9.8 %custom-call.8 = f32[1,128,128]{1,2,0:T(8,128)S(1)} custom-call(f32[1,128,128]{2,1,0:T(8,128)S(1)} %fusion.21), custom_call_target="InvertDiagBlocksLowerTriangular" | custom-call | tf_op jit(solution)/shard_map/triangular_solve/custom-call.0 | solution.py:26
  529.2 0.3 fusion.16
  529.5 13.5 %all-reduce.9.cloned.1.call-done = f32[256,128]{1,0:T(8,128)} async-done(((f32[256,128]{1,0:T(8,128)}), f32[256,128]{1,0:T(8,128)}) %all-reduce.9.cloned.1.call-update) | async-done | bytes 131088
  543.0 0.8 fusion.31
  543.8 0.2 multiply_reduce_fusion.1
  544.0 75.8 %psum.22 = f32[128]{0:T(128)S(1)} all-reduce(f32[128]{0:T(128)S(1)} %get-tuple-element.553), channel_id=1, replica_groups=mesh['ia'=8,'ja'=8,'ka'=4] {'ia','ja','ka'}, use_global_device_ids=true, to_apply=%region_16.19 | all-reduce | flops 128 | bytes 1024 | tf_op jit(solution)/shard_map/psum | solution.py:78
  619.9 0.9 fusion.48
  620.9 0.6 dynamic-slice.4
  622.1 34.9 %all_gather.40 = f32[256,128]{1,0:T(8,128)S(1)} all-gather(f32[8,128]{1,0:T(8,128)S(1)} %broadcast_multiply_fusion.1), channel_id=1, replica_groups=mesh['ia'=8,'ja'=8,'ka'=4] {'ia','ka'}, dimensions={0}, use_global_device_ids=true | all-gather | bytes 135168 | tf_op jit(solution)/shard_map/all_gather | solution.py:52
  657.1 0.5 convolution_bitcast_fusion
  657.6 1.6 while.44
  659.2 0.7 copy-done.2
  659.9 83.7 %all-gather.15.cloned.1.call-done = f32[32768,128]{1,0:T(8,128)} async-done(((f32[128,128]{1,0:T(8,128)}), f32[32768,128]{1,0:T(8,128)}) %all-gather.15.cloned.1.call-update) | async-done | bytes 16777232 | tf_op jit(solution)/shard_map/all_gather | solution.py:41
  743.6 6.6 reduce_sum.92
  750.4 0.6 select_reduce_fusion.3
  751.7 0.1 copy.17
  751.8 11.7 %cholesky.81 = f32[128,128]{1,0:T(8,128)S(1)} custom-call(f32[128,128]{1,0:T(8,128)S(1)} %fusion.24), custom_call_target="Cholesky" | custom-call | tf_op jit(solution)/shard_map/jit(cholesky)/cholesky | solution.py:23
  763.5 0.6 compare_reduce_fusion
  764.2 0.7 fusion.22
  764.8 9.8 %custom-call.9 = f32[1,128,128]{1,2,0:T(8,128)S(1)} custom-call(f32[1,128,128]{2,1,0:T(8,128)S(1)} %fusion.22), custom_call_target="InvertDiagBlocksLowerTriangular" | custom-call | tf_op jit(solution)/shard_map/triangular_solve/custom-call.0 | solution.py:26
  774.7 0.3 fusion.14
  774.9 65.4 %all-reduce.11.cloned.1.call-done = f32[512,128]{1,0:T(8,128)} async-done(((f32[512,128]{1,0:T(8,128)}), f32[512,128]{1,0:T(8,128)}) %all-reduce.11.cloned.1.call-update) | async-done | bytes 262160
  840.3 0.8 fusion.29
  841.2 0.2 multiply_reduce_fusion
  841.4 75.0 %psum.23 = f32[128]{0:T(128)S(1)} all-reduce(f32[128]{0:T(128)S(1)} %get-tuple-element.555), channel_id=1, replica_groups=mesh['ia'=8,'ja'=8,'ka'=4] {'ia','ja','ka'}, use_global_device_ids=true, to_apply=%region_23.26 | all-reduce | flops 128 | bytes 1024 | tf_op jit(solution)/shard_map/psum | solution.py:78
  916.4 45.3 %all_gather.43 = f32[512,128]{1,0:T(8,128)S(1)} all-gather(f32[8,128]{1,0:T(8,128)S(1)} %broadcast_multiply_fusion), channel_id=1, replica_groups=mesh['ia'=8,'ja'=8,'ka'=4] {'ia','ja'}, dimensions={0}, use_global_device_ids=true | all-gather | bytes 266240 | tf_op jit(solution)/shard_map/all_gather | solution.py:55
  961.7 0.7 copy.54
  962.4 0.7 copy.55
  963.0 0.7 copy.56
  (58 shorter events, 1.2 us)
Async XLA Ops:
  8.0 1.9 copy-start
  8.0 11.1 %copy-start.8 = (u32[256]{0:T(256)S(1)}, u32[256]{0:T(256)}, u32[]{:S(2)}) copy-start(u32[256]{0:T(256)} %constant.196) | copy-start | bytes 3076
  8.0 133.7 %all-gather.9.cloned.1.call-start = ((), (), s32[]{:S(2)}) async-start(), calls=%async_computation | async-start | bytes 16842752 | tf_op jit(solution)/shard_map/all_gather | solution.py:41
  9.8 258.5 %all-gather.11.cloned.1.call-start = ((), (), s32[]{:S(2)}) async-start(), calls=%async_computation.1 | async-start | bytes 16842752 | tf_op jit(solution)/shard_map/all_gather | solution.py:41
  10.8 288.9 %all-reduce.7.cloned.1.call-start = ((), (), s32[]{:S(2)}) async-start(), calls=%async_computation.4 | async-start | bytes 262144
  18.4 0.7 copy-start.3
  19.1 479.1 %all-gather.13.cloned.1.call-start = ((), (), s32[]{:S(2)}) async-start(), calls=%async_computation.2 | async-start | bytes 16842752 | tf_op jit(solution)/shard_map/all_gather | solution.py:41
  268.3 107.9 %copy-start.7 = (u32[256]{0:T(256)S(1)}, u32[256]{0:T(256)}, u32[]{:S(2)}) copy-start(u32[256]{0:T(256)} %constant.200) | copy-start | bytes 3076
  268.3 150.9 %copy-start.5 = (bf16[1,64,64,128]{3,2,1,0:T(8,128)(2,1)S(1)}, bf16[1,64,64,128]{3,2,1,0:T(8,128)(2,1)}, u32[]{:S(2)}) copy-start(bf16[1,64,64,128]{3,2,1,0:T(8,128)(2,1)} %param.14) | copy-start | bytes 3145732
  376.1 166.8 %all-reduce.9.cloned.1.call-start = ((), (), s32[]{:S(2)}) async-start(), calls=%async_computation.5 | async-start | bytes 262144
  421.0 0.7 copy-start.4
  421.7 321.9 %all-gather.15.cloned.1.call-start = ((), (), s32[]{:S(2)}) async-start(), calls=%async_computation.3 | async-start | bytes 16842752 | tf_op jit(solution)/shard_map/all_gather | solution.py:41
  498.2 122.7 %copy-start.6 = (u32[256]{0:T(256)S(1)}, u32[256]{0:T(256)}, u32[]{:S(2)}) copy-start(u32[256]{0:T(256)} %constant.204) | copy-start | bytes 3076
  620.8 219.5 %all-reduce.11.cloned.1.call-start = ((), (), s32[]{:S(2)}) async-start(), calls=%async_computation.6 | async-start | bytes 524288
  659.2 0.7 copy-start.2
  743.6 220.1 %copy-start.1 = (f32[512,128]{1,0:T(8,128)S(1)}, f32[512,128]{1,0:T(8,128)}, u32[]{:S(2)}) copy-start(f32[512,128]{1,0:T(8,128)} %param.18) | copy-start | bytes 786436
Sparse Core Ops, SparseCore 0:
  13.1 128.5 all-gather.8
  146.1 122.2 all-gather.10
  376.3 121.8 all-gather.12
  621.0 122.6 all-gather.14
Sparse Core Ops, SparseCore 1:
  19.2 155.4 all-reduce.6
  421.8 121.1 all-reduce.8
  660.0 180.3 all-reduce.10
